TPU v7x, 128 devices: a whole 4x4x4 slice. The times are simulated.
128 devices in a mesh: req: 16 (over z, y), kv: 8 (over x, core).
Axes of the slice: x: 4, y: 4, z: 4, core: 2. Of those that a mesh axis runs over, the one named last changes fastest.
Arguments:
- hidden_in: bfloat16 [16384, 2048], P(('req', 'kv')), may hold values from -6 to 6
- slot_tokens: int32 [16384], replicated, may hold values from 0 to 16383, as said below
- cache_len: int32 [128], P('req'), may hold values from 1 to 2048, 65536 in all
- prefill_start: int32 [16], P('req'), may hold values from 0 to 2048
- key_cache: bfloat16 [128, 2048, 1024], P('req', None, 'kv')
- value_cache: bfloat16 [128, 2048, 1024], P('req', None, 'kv'), may hold values from -18 to 18
- key_prefix: bfloat16 [16, 2048, 1024], P('req', None, 'kv')
- value_prefix: bfloat16 [16, 2048, 1024], P('req', None, 'kv'), may hold values from -18 to 18
- attn_gain: float32 [2048], replicated, may hold values from 0.25 to 1.75
- q_proj: bfloat16 [2048, 2048], P(None, 'kv'), may hold values from -0.125 to 0.125
- k_proj: bfloat16 [2048, 1024], P(None, 'kv'), may hold values from -0.125 to 0.125
- v_proj: bfloat16 [2048, 1024], P(None, 'kv'), may hold values from -0.125 to 0.125
- q_gain: float32 [128], replicated, may hold values from 0.25 to 1.75
- k_gain: float32 [128], replicated, may hold values from 0.25 to 1.75
- o_proj: bfloat16 [2048, 2048], P('kv'), may hold values from -0.125 to 0.125
- ffn_gain: float32 [2048], replicated, may hold values from 0.25 to 1.75
- w_gate: bfloat16 [2048, 6144], P(None, 'req'), may hold values from -0.125 to 0.125
- w_up: bfloat16 [2048, 6144], P(None, 'req'), may hold values from -0.125 to 0.125
- w_down: bfloat16 [6144, 2048], P('req'), may hold values from -0.078125 to 0.078125
- final_gain: float32 [2048], replicated, may hold values from 0.25 to 1.75
- lm_head: bfloat16 [2048, 151936], P(None, ('req', 'kv')), may hold values from -0.375 to 0.375
Outputs:
- layer_out: bfloat16 [16384, 2048], P(('req', 'kv'))
- max_logit: float32 [144], replicated
Inputs may be any that keep to these rules, and one draw needn't show every extreme that they name: slot_tokens is a permutation of the batch's tokens; each device's 128 consecutive slots take exactly 1 token from each device's 128 consecutive batch tokens.
All inputs are finite; a program needn't handle non-finite values. No bound on the sum of `cache_len` on one device may be relied on, other than what follows from the above.
Results may differ from a plain program's by a relative error of at most 0.0085.
The roundings to bfloat16 on the way count: a program that leaves them out, or rounds other values in their place, can miss the bound.
Values may be sent and summed in bfloat16 or wider, within the bound.
A program may use at most 128 MiB of HBM per device.

v0:
```python
import jax
import jax.numpy as jnp
from jax import lax
from jax.sharding import PartitionSpec as P

EPS = 1e-06
NEG = -1e30


def spread(value, axis, root):
    mine = lax.axis_index(axis) == root
    return lax.psum(jnp.where(mine, value, jnp.zeros_like(value)), axis)


def norm_rows(values, gain_vec):
    wide = values.astype(jnp.float32)
    return wide * lax.rsqrt(jnp.mean(wide * wide, axis=-1, keepdims=True) + EPS) * gain_vec


def rotate(values, places):
    half_dim = values.shape[-1] // 2
    freqs = 1000000.0 ** (-(jnp.arange(half_dim, dtype=jnp.float32) * 2.0 / values.shape[-1]))
    angles = places[:, None] * freqs[None, :]
    cosine = jnp.cos(angles)[:, None, :]
    sine = jnp.sin(angles)[:, None, :]
    first_half = values[..., :half_dim]
    second_half = values[..., half_dim:]
    return jnp.concatenate(
        [first_half * cosine - second_half * sine, second_half * cosine + first_half * sine],
        axis=-1,
    )


def prefill_full(q_heads, key_old, value_old, key_new, value_new, start_at):
    old_len = key_old.shape[0]
    fresh_rows = q_heads.shape[0]
    factor = q_heads.shape[-1] ** (-0.5)
    all_keys = jnp.concatenate([key_old, key_new], axis=0)
    all_values = jnp.concatenate([value_old, value_new], axis=0)
    scores = (
        jnp.einsum("cgd,kd->gck", q_heads, all_keys, preferred_element_type=jnp.float32) * factor
    )
    key_index = jnp.arange(old_len + fresh_rows, dtype=jnp.int32)[None, :]
    row_index = jnp.arange(fresh_rows, dtype=jnp.int32)[:, None]
    allowed = jnp.where(key_index < old_len, key_index < start_at, key_index - old_len <= row_index)
    scores = jnp.where(allowed[None], scores, NEG)
    row_peak = jnp.max(scores, axis=-1, keepdims=True)
    expd = jnp.exp(scores - row_peak)
    weights = (expd / jnp.sum(expd, axis=-1, keepdims=True)).astype(jnp.bfloat16)
    return jnp.einsum(
        "gck,kd->cgd", weights, all_values, preferred_element_type=jnp.float32
    ).astype(jnp.bfloat16)


def decode_attend(q_heads, key_old, value_old, key_self, value_self, lengths):
    factor = q_heads.shape[-1] ** (-0.5)
    past = jnp.einsum("bgd,bld->bgl", q_heads, key_old, preferred_element_type=jnp.float32) * factor
    slot_index = jnp.arange(key_old.shape[1], dtype=jnp.int32)
    past = jnp.where(slot_index[None, None, :] < lengths[:, None, None], past, NEG)
    own_score = (
        jnp.einsum("bgd,bd->bg", q_heads, key_self, preferred_element_type=jnp.float32) * factor
    )
    row_peak = jnp.maximum(jnp.max(past, axis=-1), own_score)
    past_exp = jnp.exp(past - row_peak[..., None])
    own_exp = jnp.exp(own_score - row_peak)
    row_total = jnp.sum(past_exp, axis=-1) + own_exp
    past_w = (past_exp / row_total[..., None]).astype(jnp.bfloat16)
    own_w = (own_exp / row_total).astype(jnp.bfloat16)
    summed = jnp.einsum("bgl,bld->bgd", past_w, value_old, preferred_element_type=jnp.float32)
    summed = (
        summed + own_w.astype(jnp.float32)[..., None] * value_self.astype(jnp.float32)[:, None, :]
    )
    return summed.astype(jnp.bfloat16)


def butterfly(value, axis, combine):
    size = lax.axis_size(axis)
    step = 1
    while step < size:
        pairs = [(i, i ^ step) for i in range(size)]
        value = combine(value, lax.ppermute(value, axis, pairs))
        step *= 2
    return value


def butterfly_gather(value, axis):
    size = lax.axis_size(axis)
    me = lax.axis_index(axis)
    step = 1
    while step < size:
        pairs = [(i, i ^ step) for i in range(size)]
        other = lax.ppermute(value, axis, pairs)
        low = me // step % 2 == 0
        value = jnp.concatenate(
            [jnp.where(low, value, other), jnp.where(low, other, value)], axis=0
        )
        step *= 2
    return value


def radix_exchange(value, axis, step, radix):
    size = lax.axis_size(axis)
    got = [value]
    for digit in range(1, radix):
        pairs = [(i, i ^ digit * step) for i in range(size)]
        got.append(lax.ppermute(value, axis, pairs))
    return got


def radix_reduce(value, axis, combine, radix):
    size = lax.axis_size(axis)
    step = 1
    while step < size:
        for other in radix_exchange(value, axis, step, radix)[1:]:
            value = combine(value, other)
        step *= radix
    return value


def radix_gather(value, axis, radix):
    size = lax.axis_size(axis)
    me = lax.axis_index(axis)
    step = 1
    while step < size:
        got = radix_exchange(value, axis, step, radix)
        order = jnp.arange(radix, dtype=jnp.int32) ^ me // step % radix
        value = jnp.stack(got)[order].reshape((radix * value.shape[0],) + value.shape[1:])
        step *= radix
    return value


def mixed_reduce(value, axis, combine, radices):
    me = lax.axis_index(axis)
    step = 1
    for radix in radices:
        got = radix_exchange(value, axis, step, radix)
        order = jnp.arange(radix, dtype=jnp.int32) ^ me // step % radix
        members = jnp.stack(got)[order]
        while members.shape[0] > 1:
            members = combine(members[0::2], members[1::2])
        value = members[0]
        step *= radix
    return value


def regroup(rows_in):
    return lax.all_to_all(rows_in, ("req", "kv"), split_axis=0, concat_axis=0, tiled=True)


def shards(
    hidden_in,
    slot_tokens,
    cache_len,
    prefill_start,
    key_cache,
    value_cache,
    key_prefix,
    value_prefix,
    attn_gain,
    q_proj,
    k_proj,
    v_proj,
    q_gain,
    k_gain,
    o_proj,
    ffn_gain,
    w_gate,
    w_up,
    w_down,
    final_gain,
    lm_head,
):
    req_count = lax.axis_size("req")
    kv_count = lax.axis_size("kv")
    devices = req_count * kv_count
    rows_dev = hidden_in.shape[0]
    kv_index = lax.axis_index("kv")
    self_index = lax.axis_index("req") * kv_count + kv_index
    slot_table = slot_tokens.reshape(devices, rows_dev)
    from_self = slot_table // rows_dev == self_index
    send_rows = jnp.sum(jnp.where(from_self, slot_table - self_index * rows_dev, 0), axis=1)
    slot_place = lax.dynamic_index_in_dim(slot_table, self_index, 0, keepdims=False) // rows_dev
    arrived = regroup(hidden_in[send_rows])
    owner_rows = arrived[slot_place]
    rows_all = lax.all_gather(owner_rows, "kv", axis=0, tiled=True)
    normed = norm_rows(rows_all, attn_gain).astype(jnp.bfloat16)
    o_full = lax.all_to_all(
        jnp.broadcast_to(o_proj[None], (kv_count,) + o_proj.shape),
        "kv",
        split_axis=0,
        concat_axis=0,
        tiled=True,
    ).reshape(kv_count * o_proj.shape[0], o_proj.shape[1])
    ff_dev = w_gate.shape[1]
    ff_piece = ff_dev // kv_count
    weight_piece = jnp.stack(
        [
            lax.dynamic_slice_in_dim(w_gate, kv_index * ff_piece, ff_piece, axis=1).T,
            lax.dynamic_slice_in_dim(w_up, kv_index * ff_piece, ff_piece, axis=1).T,
            lax.dynamic_slice_in_dim(w_down, kv_index * ff_piece, ff_piece, axis=0),
        ]
    )
    weight_all = lax.all_gather(weight_piece, "req", axis=1, tiled=True)
    model_dim = w_gate.shape[0]
    q_cols = q_proj.shape[1]
    kv_cols = k_proj.shape[1]
    projected = jnp.concatenate(
        [
            jnp.dot(normed, q_proj, preferred_element_type=jnp.float32),
            jnp.dot(normed, k_proj, preferred_element_type=jnp.float32),
            jnp.dot(normed, v_proj, preferred_element_type=jnp.float32),
        ],
        axis=1,
    )
    tok_req = projected.shape[0]
    head_dim = q_gain.shape[0]
    dec_count = cache_len.shape[0]
    fresh_count = tok_req - dec_count
    q_raw = projected[:, :q_cols].reshape(tok_req, q_cols // head_dim, head_dim)
    k_raw = projected[:, q_cols : q_cols + kv_cols].reshape(tok_req, kv_cols // head_dim, head_dim)
    v_new = (
        projected[:, q_cols + kv_cols :]
        .astype(jnp.bfloat16)
        .reshape(tok_req, kv_cols // head_dim, head_dim)
    )
    places = jnp.concatenate(
        [prefill_start[0] + jnp.arange(fresh_count, dtype=jnp.int32), cache_len]
    ).astype(jnp.float32)
    queries = rotate(norm_rows(q_raw, q_gain), places).astype(jnp.bfloat16)
    keys_new = rotate(norm_rows(k_raw, k_gain), places).astype(jnp.bfloat16)
    pre_out = prefill_full(
        queries[:fresh_count],
        key_prefix[0, :, 0:head_dim],
        value_prefix[0, :, 0:head_dim],
        keys_new[:fresh_count, 0],
        v_new[:fresh_count, 0],
        prefill_start[0],
    )
    dec_out = decode_attend(
        queries[fresh_count:],
        key_cache,
        value_cache,
        keys_new[fresh_count:, 0],
        v_new[fresh_count:, 0],
        cache_len,
    )
    pieces = jnp.concatenate([pre_out, dec_out], axis=0)
    pieces, weight_all, o_full = lax.optimization_barrier((pieces, weight_all, o_full))
    gate_w = weight_all[0]
    up_w = weight_all[1]
    down_w = weight_all[2]
    attended = lax.all_gather(pieces.reshape(tok_req, q_cols), "kv", axis=1, tiled=True)
    resid = (
        rows_all.astype(jnp.float32) + jnp.dot(attended, o_full, preferred_element_type=jnp.float32)
    ).astype(jnp.bfloat16)
    ffn_in = norm_rows(resid, ffn_gain).astype(jnp.bfloat16)
    contract_last = (((1,), (1,)), ((), ()))
    gate_part = lax.dot_general(ffn_in, gate_w, contract_last, preferred_element_type=jnp.float32)
    up_part = lax.dot_general(ffn_in, up_w, contract_last, preferred_element_type=jnp.float32)
    hidden_act = (jax.nn.silu(gate_part) * up_part).astype(jnp.bfloat16)
    tail_count = tok_req - fresh_count + 1
    tail_pad = -(-tail_count // 8) * 8
    down_part = jnp.dot(hidden_act, down_w, preferred_element_type=jnp.float32)
    ffn_part = lax.psum_scatter(down_part, "kv", scatter_dimension=0, tiled=True)
    tail_part = jnp.dot(
        hidden_act[tok_req - tail_pad :], down_w, preferred_element_type=jnp.float32
    )
    tail_sum = mixed_reduce(tail_part, "kv", jnp.add, (2, 4))[tail_pad - tail_count :]
    tail_out = (resid[fresh_count - 1 :].astype(jnp.float32) + tail_sum).astype(jnp.bfloat16)
    tail_rows = norm_rows(tail_out, final_gain).astype(jnp.bfloat16)
    local_peaks = jnp.max(
        jnp.dot(radix_gather(tail_rows, "req", 4), lm_head, preferred_element_type=jnp.float32),
        axis=1,
    )
    max_logit = radix_reduce(
        mixed_reduce(local_peaks, "kv", jnp.maximum, (2, 4)), "req", jnp.maximum, 4
    )
    ffn_part, max_logit = lax.optimization_barrier((ffn_part, max_logit))
    mine = lax.dynamic_slice_in_dim(resid, kv_index * rows_dev, rows_dev, axis=0)
    out_rows = (mine.astype(jnp.float32) + ffn_part).astype(jnp.bfloat16)
    going_back = jnp.zeros_like(out_rows).at[slot_place].set(out_rows)
    returned = regroup(going_back)
    layer_out = jnp.zeros_like(hidden_in).at[send_rows].set(returned)
    return (layer_out, max_logit)


def solution(mesh):
    placed = (
        P(("req", "kv"), None),
        P(),
        P("req"),
        P("req"),
        P("req", None, "kv"),
        P("req", None, "kv"),
        P("req", None, "kv"),
        P("req", None, "kv"),
        P(),
        P(None, "kv"),
        P(None, "kv"),
        P(None, "kv"),
        P(),
        P(),
        P("kv", None),
        P(),
        P(None, "req"),
        P(None, "req"),
        P("req", None),
        P(),
        P(None, ("req", "kv")),
    )
    return jax.shard_map(
        shards, mesh=mesh, in_specs=placed, out_specs=(P(("req", "kv"), None), P()), check_vma=False
    )
```

profile of v0, /device:TPU:1, one launch (start us, length us, event | category | flops | bytes accessed | tf_op | source)
XLA Modules:
  0.0 336.4 jit_solution(1163954709671219122)
XLA Ops:
  8.3 2.6 gather_fusion
  13.5 11.5 %all-to-all-start = ((bf16[128,2,1024]{2,1,0:T(2,128)(2,1)}), bf16[128,2,1024]{2,1,0:T(2,128)(2,1)S(1)}, u32[]{:S(2)}, u32[]{:S(2)}) async-start(bf16[128,2,1024]{2,1,0:T(2,128)(2,1)} %reshape.574), calls=%async_computation | async-start | bytes 1048576 | tf_op jit(solution)/shard_map/all_to_all | solution.py:147
  25.8 13.0 %all-to-all-done = bf16[128,2,1024]{2,1,0:T(2,128)(2,1)S(1)} async-done(((bf16[128,2,1024]{2,1,0:T(2,128)(2,1)}), bf16[128,2,1024]{2,1,0:T(2,128)(2,1)S(1)}, u32[]{:S(2)}, u32[]{:S(2)}) %all-to-all-start) | async-done | bytes 524320 | tf_op jit(solution)/shard_map/all_to_all | solution.py:147
  39.5 1.7 gather_fusion.1
  41.3 1.9 constant_dynamic-slice_fusion
  44.6 5.6 %broadcast_in_dim.46 = bf16[8,256,2048]{2,1,0:T(8,128)(2,1)} broadcast(bf16[256,2048]{1,0:T(8,128)(2,1)} %param.35), dimensions={1,2} | broadcast | bytes 9437184 | tf_op jit(solution)/shard_map/broadcast_in_dim | solution.py:188
  50.2 5.8 %all-to-all-start.1 = ((bf16[8,256,2048]{2,1,0:T(8,128)(2,1)}), bf16[8,256,2048]{2,1,0:T(8,128)(2,1)}, u32[]{:S(2)}, u32[]{:S(2)}) async-start(bf16[8,256,2048]{2,1,0:T(8,128)(2,1)} %broadcast_in_dim.46), calls=%async_computation.1 | async-start | bytes 16777216 | tf_op jit(solution)/shard_map/all_to_all | solution.py:187
  57.0 1.9 multiply_cosine_fusion
  59.0 4.0 %fusion.4 = pred[1016,3064]{1,0:T(8,128)(4,1)} fusion(s32[3064]{0:T(1024)S(1)} %iota_add_fusion, pred[3064]{0:T(1024)(128)(4,1)S(1)} %get-tuple-element.34, pred[3064]{0:T(1024)(128)(4,1)S(1)} %get-tuple-element.35), kind=kLoop, calls=%fused_computation.21 | loop fusion | flops 6226048 | bytes 3131408 | tf_op jit(solution)/shard_map/jit(_where)/select_n | solution.py:45
  63.1 23.5 %all-gather.9.cloned.1.call-done = bf16[1024,2048]{1,0:T(8,128)(2,1)} async-done(((bf16[128,2048]{1,0:T(8,128)(2,1)}), bf16[1024,2048]{1,0:T(8,128)(2,1)}) %all-gather.9.cloned.1.call-update) | async-done | bytes 4194320 | tf_op jit(solution)/shard_map/all_gather | solution.py:185
  86.6 3.2 fusion.10
  91.3 2.3 multiply_reduce_fusion
  93.6 1.6 copy.50
  95.2 3.7 %multiply_reduce_fusion.1 = (f32[1024]{0:T(1024)S(1)}, f32[1024,128]{0,1:T(8,128)S(1)}) fusion(bf16[1024,2048]{1,0:T(8,128)(2,1)} %copy-done.3, bf16[2048,128]{1,0:T(8,128)(2,1)S(1)} %copy-done.6), kind=kOutput, calls=%fused_computation.77 | convolution fusion | flops 537132032 | bytes 5246976 | tf_op jit(solution)/shard_map/dot_general | solution.py:210
  99.1 1.4 fusion.49
  102.8 1.3 fusion.95
  104.7 3.9 %convolution_convert_fusion = bf16[1024,128]{1,0:T(8,128)(2,1)S(1)} fusion(bf16[1024,2048]{1,0:T(8,128)(2,1)} %copy-done.3, bf16[2048,128]{1,0:T(8,128)(2,1)S(1)} %copy-done.14), kind=kOutput, calls=%fused_computation.51 | convolution fusion | flops 537001984 | bytes 4980736 | tf_op jit(solution)/shard_map/dot_general | solution.py:211
  109.5 15.9 %fusion.96 = (f32[2,1016]{1,0:T(2,128)S(1)}, f32[2,1016,3064]{2,1,0:T(8,128)}) fusion(pred[1016,3064]{1,0:T(8,128)(4,1)} %fusion.4, bf16[1016,128]{1,0:T(8,128)(2,1)S(1)} %copy.49, bf16[2048,128]{1,0:T(8,128)(2,1)S(1)} %bitcast.175, bf16[1024,2,64]{2,0,1:T(8,128)(2,1)S(1)} %get-tuple-element.14, bf16[1024,2,64]{2,0,1:T(8,128)(2,1)S(1)} %get-tuple-element.15), kind=kOutput, calls=%fused_computation.188 | convolution fusion | flops 1621384704 | bytes 29334016 | tf_op jit(solution)/shard_map/sub | solution.py:48
  125.4 12.3 %fusion.32 = bf16[1016,2,128]{2,0,1:T(8,128)(2,1)S(1)} fusion(f32[2,1016,3064]{2,1,0:T(8,128)} %get-tuple-element.31, f32[2,1016]{1,0:T(2,128)S(1)} %get-tuple-element.30, bf16[1016,128]{1,0:T(8,128)(2,1)S(1)} %slice.142, bf16[2048,128]{1,0:T(8,128)(2,1)S(1)} %bitcast.176), kind=kOutput, calls=%fused_computation.50 | convolution fusion | flops 1608149248 | bytes 26216896 | tf_op jit(solution)/shard_map/gck,kd->cgd/dot_general | solution.py:50
  137.8 20.7 %all-to-all-done.1 = bf16[8,256,2048]{2,1,0:T(8,128)(2,1)} async-done(((bf16[8,256,2048]{2,1,0:T(8,128)(2,1)}), bf16[8,256,2048]{2,1,0:T(8,128)(2,1)}, u32[]{:S(2)}, u32[]{:S(2)}) %all-to-all-start.1) | async-done | bytes 8388640 | tf_op jit(solution)/shard_map/all_to_all | solution.py:187
  158.4 12.4 %all-gather.5.cloned.1.call-done = bf16[3,768,2048]{2,1,0:T(8,128)(2,1)} async-done(((bf16[3,48,2048]{2,1,0:T(8,128)(2,1)}), bf16[3,768,2048]{2,1,0:T(8,128)(2,1)}) %all-gather.5.cloned.1.call-update) | async-done | bytes 9437200 | tf_op jit(solution)/shard_map/all_gather | solution.py:203
  171.9 33.3 %all-gather.7.cloned.1.call-done = bf16[1024,2048]{0,1:T(8,128)(2,1)} async-done(((bf16[1024,256]{0,1:T(8,128)(2,1)}), bf16[1024,2048]{0,1:T(8,128)(2,1)}) %all-gather.7.cloned.1.call-update) | async-done | bytes 4194320 | tf_op jit(solution)/shard_map/all_gather | solution.py:252
  205.2 14.6 %fusion.7 = (f32[1024]{0:T(1024)S(1)}, bf16[1024,2048]{1,0:T(8,128)(2,1)S(1)}) fusion(bf16[1024,2048]{0,1:T(8,128)(2,1)} %all-gather.7.cloned.1.call-done, bf16[2048,2048]{1,0:T(8,128)(2,1)} %bitcast.25, bf16[1024,2048]{1,0:T(8,128)(2,1)} %all-gather.9.cloned.1.call-done), kind=kOutput, calls=%fused_computation.26 | convolution fusion | flops 8602516480 | bytes 20975616 | tf_op jit(solution)/shard_map/dot_general | solution.py:254
  219.9 7.0 %fusion.18 = f32[1024,768]{1,0:T(8,128)S(1)} fusion(bf16[3,768,2048]{2,1,0:T(8,128)(2,1)} %all-gather.5.cloned.1.call-done, bf16[1024,2048]{1,0:T(8,128)(2,1)S(1)} %get-tuple-element.33, f32[2048]{0:T(1024)S(1)} %copy-done.17, f32[1024]{0:T(1024)S(1)} %add_rsqrt_fusion.1), kind=kOutput, calls=%fused_computation.37 | convolution fusion | flops 3229614080 | bytes 10498048 | tf_op jit(solution)/shard_map/dot_general | solution.py:259
  227.0 3.9 %multiply_convert_fusion = bf16[1024,768]{1,0:T(8,128)(2,1)S(1)} fusion(f32[1024,768]{1,0:T(8,128)S(1)} %fusion.18, bf16[3,768,2048]{2,1,0:T(8,128)(2,1)S(1)} %bitcast.145, bf16[1024,2048]{1,0:T(8,128)(2,1)S(1)} %get-tuple-element.33, f32[2048]{0:T(1024)S(1)} %copy-done.17, f32[1024]{0:T(1024)S(1)} %add_rsqrt_fusion.1), kind=kOutput, calls=%fused_computation.41 | convolution fusion | flops 3234332672 | bytes 12070912 | tf_op jit(solution)/shard_map/dot_general | solution.py:258
  230.9 5.6 %fusion.16 = f32[1024,2048]{1,0:T(8,128)} fusion(bf16[1024,768]{1,0:T(8,128)(2,1)S(1)} %multiply_convert_fusion, bf16[3,768,2048]{2,1,0:T(8,128)(2,1)S(1)} %bitcast.145), kind=kOutput, calls=%fused_computation.35 | convolution fusion | flops 3221225472 | bytes 13107200 | tf_op jit(solution)/shard_map/dot_general | solution.py:263
  236.7 2.4 fusion.14
  241.8 1.4 collective-permute-start.2
  243.2 1.3 collective-permute-start.1
  244.6 6.2 %collective-permute-done.3 = f32[16,2048]{1,0:T(8,128)S(1)} collective-permute-done((f32[16,2048]{1,0:T(8,128)S(1)}, f32[16,2048]{1,0:T(8,128)S(1)}, u32[]{:S(2)}, u32[]{:S(2)}) %collective-permute-start.3) | collective-permute-done | bytes 131104 | tf_op jit(solution)/shard_map/ppermute | solution.py:106
  250.8 1.3 collective-permute-done.1
  253.9 2.5 collective-permute-start.6
  257.3 1.4 collective-permute-done.6
  258.7 2.4 collective-permute-done.5
  261.8 2.7 collective-permute-start.9
  265.3 3.3 collective-permute-done.9
  268.6 1.7 collective-permute-done.8
  271.2 4.3 %convolution_reduce_fusion = f32[144]{0:T(256)S(1)} fusion(bf16[144,2048]{1,0:T(8,128)(2,1)S(1)} %reshape.484, bf16[2048,1187]{0,1:T(8,128)(2,1)} %param.41), kind=kOutput, calls=%fused_computation.52 | convolution fusion | flops 700291840 | bytes 5452352 | tf_op jit(solution)/shard_map/dot_general | solution.py:272
  275.4 5.0 %collective-permute-start.10 = (f32[144]{0:T(256)S(1)}, f32[144]{0:T(256)S(1)}, u32[]{:S(2)}, u32[]{:S(2)}) collective-permute-start(f32[144]{0:T(256)S(1)} %convolution_reduce_fusion), channel_id=1, source_target_pairs={{0,1},{1,0},{2,3},{3,2},{4,5},{5,4},{6,7},{7,6},{8,9},{9,8},{10,11... | collective-permute-start | bytes 1736 | tf_op jit(solution)/shard_map/ppermute | solution.py:106
  282.0 2.0 collective-permute-start.12
  287.6 1.2 collective-permute-start.16
  289.5 1.4 collective-permute-start.14
  291.3 1.4 collective-permute-done.15
  292.7 2.1 collective-permute-start.19
  296.4 2.3 collective-permute-done.18
  299.4 2.3 scatter_custom_fusion
  303.1 23.8 %all_to_all.29 = bf16[128,2,1024]{2,1,0:T(2,128)(2,1)S(1)} all-to-all(bf16[128,2,1024]{2,1,0:T(2,128)(2,1)S(1)} %reshape.576), channel_id=1, replica_groups=mesh['req'=16,'kv'=8] {'req','kv'}, dimensions={0} | all-to-all | bytes 1048576 | tf_op jit(solution)/shard_map/all_to_all | solution.py:147
  327.3 2.4 scatter_custom_fusion.1
  (160 shorter events, 31.4 us)
Async XLA Ops:
  7.2 36.5 %copy-start = (bf16[384,2048]{1,0:T(8,128)(2,1)S(1)}, bf16[384,2048]{1,0:T(8,128)(2,1)}, u32[]{:S(2)}) copy-start(bf16[384,2048]{1,0:T(8,128)(2,1)} %param.39) | copy-start | bytes 4718596
  13.5 25.2 %all-to-all-start = ((bf16[128,2,1024]{2,1,0:T(2,128)(2,1)}), bf16[128,2,1024]{2,1,0:T(2,128)(2,1)S(1)}, u32[]{:S(2)}, u32[]{:S(2)}) async-start(bf16[128,2,1024]{2,1,0:T(2,128)(2,1)} %reshape.574), calls=%async_computation | async-start | bytes 1048576 | tf_op jit(solution)/shard_map/all_to_all | solution.py:147
  25.0 61.6 %all-gather.9.cloned.1.call-start = ((), (), s32[]{:S(2)}) async-start(), calls=%async_computation.7 | async-start | bytes 4718592 | tf_op jit(solution)/shard_map/all_gather | solution.py:185
  41.3 129.5 %all-gather.5.cloned.1.call-start = ((), (), s32[]{:S(2)}) async-start(), calls=%async_computation.4 | async-start | bytes 10027008 | tf_op jit(solution)/shard_map/all_gather | solution.py:203
  50.2 6.7 %copy-start.10 = (s32[8]{0:T(128)S(1)}, s32[8]{0:T(128)}, u32[]{:S(2)}) copy-start(s32[8]{0:T(128)} %param.23) | copy-start | bytes 100
  50.2 108.2 %all-to-all-start.1 = ((bf16[8,256,2048]{2,1,0:T(8,128)(2,1)}), bf16[8,256,2048]{2,1,0:T(8,128)(2,1)}, u32[]{:S(2)}, u32[]{:S(2)}) async-start(bf16[8,256,2048]{2,1,0:T(8,128)(2,1)} %broadcast_in_dim.46), calls=%async_computation.1 | async-start | bytes 16777216 | tf_op jit(solution)/shard_map/all_to_all | solution.py:187
  56.1 149.1 %all-gather.7.cloned.1.call-start = ((), (), s32[]{:S(2)}) async-start(), calls=%async_computation.5 | async-start | bytes 4718592 | tf_op jit(solution)/shard_map/all_gather | solution.py:252
  57.0 32.8 %copy-start.9 = (f32[2048]{0:T(1024)S(1)}, f32[2048]{0:T(1024)}, u32[]{:S(2)}) copy-start(f32[2048]{0:T(1024)} %param.29) | copy-start | bytes 24580
  86.6 3.4 %copy-start.2 = (bf16[1024,2048]{1,0:T(8,128)(2,1)S(1)}, bf16[1024,2048]{1,0:T(8,128)(2,1)}, u32[]{:S(2)}) copy-start(bf16[1024,2048]{1,0:T(8,128)(2,1)} %all-gather.9.cloned.1.call-done) | copy-start | bytes 12582916
  90.0 1.2 copy-start.13
  91.3 2.3 copy-start.3
  91.3 3.9 %copy-start.6 = (bf16[2048,128]{1,0:T(8,128)(2,1)S(1)}, bf16[2048,128]{1,0:T(8,128)(2,1)}, u32[]{:S(2)}) copy-start(bf16[2048,128]{1,0:T(8,128)(2,1)} %param.31) | copy-start | bytes 1572868
  93.6 5.3 %copy-start.11 = (f32[128]{0:T(128)S(1)}, f32[128]{0:T(128)}, u32[]{:S(2)}) copy-start(f32[128]{0:T(128)} %param.34) | copy-start | bytes 1540
  95.2 5.4 %copy-start.12 = (f32[128]{0:T(128)S(1)}, f32[128]{0:T(128)}, u32[]{:S(2)}) copy-start(f32[128]{0:T(128)} %param.33) | copy-start | bytes 1540
  100.6 2.2 copy-start.4
  101.5 3.2 copy-start.14
  104.7 4.0 %copy-start.5 = (bf16[8,2048,128]{2,1,0:T(8,128)(2,1)S(1)}, bf16[8,2048,128]{2,1,0:T(8,128)(2,1)}, u32[]{:S(2)}) copy-start(bf16[8,2048,128]{2,1,0:T(8,128)(2,1)} %param.26) | copy-start | bytes 12582916
  104.7 4.8 %copy-start.15 = (bf16[1,2048,128]{2,1,0:T(8,128)(2,1)S(1)}, bf16[1,2048,128]{2,1,0:T(8,128)(2,1)}, u32[]{:S(2)}) copy-start(bf16[1,2048,128]{2,1,0:T(8,128)(2,1)} %param.27) | copy-start | bytes 1572868
  109.5 15.9 %copy-start.16 = (bf16[1,2048,128]{2,1,0:T(8,128)(2,1)S(1)}, bf16[1,2048,128]{2,1,0:T(8,128)(2,1)}, u32[]{:S(2)}) copy-start(bf16[1,2048,128]{2,1,0:T(8,128)(2,1)} %param.28) | copy-start | bytes 1572868
  171.8 48.0 %copy-start.17 = (f32[2048]{0:T(1024)S(1)}, f32[2048]{0:T(1024)}, u32[]{:S(2)}) copy-start(f32[2048]{0:T(1024)} %param.36) | copy-start | bytes 24580
  171.9 127.5 %reduce-scatter.2.cloned.1.call-start = ((), (), s32[]{:S(2)}) async-start(), calls=%async_computation.6 | async-start | bytes 9437184 | tf_op jit(solution)/shard_map/reduce_scatter | solution.py:264
  205.2 21.7 %slice-start = ((s8[9437184]{0:T(1024)(128)(4,1)}), s8[1048576]{0:T(1024)(128)(4,1)S(1)}, s32[]{:S(2)}) async-start(s8[9437184]{0:T(1024)(128)(4,1)} %bitcast.144), calls=%async_computation.8 | async-start | bytes 2097152
  205.2 21.7 %slice-start.1 = ((s8[9437184]{0:T(1024)(128)(4,1)}), s8[4194304]{0:T(1024)(128)(4,1)S(1)}, s32[]{:S(2)}) async-start(s8[9437184]{0:T(1024)(128)(4,1)} %bitcast.144), calls=%async_computation.9 | async-start | bytes 8388608
  219.9 7.1 %copy-start.7 = (bf16[1024,2048]{1,0:T(8,128)(2,1)}, bf16[1024,2048]{1,0:T(8,128)(2,1)S(1)}, u32[]{:S(2)}) copy-start(bf16[1024,2048]{1,0:T(8,128)(2,1)S(1)} %get-tuple-element.33) | copy-start | bytes 12582916
  219.9 7.1 %slice-start.2 = ((s8[9437184]{0:T(1024)(128)(4,1)}), s8[4194304]{0:T(1024)(128)(4,1)S(1)}, s32[]{:S(2)}) async-start(s8[9437184]{0:T(1024)(128)(4,1)} %bitcast.144), calls=%async_computation.10 | async-start | bytes 8388608
  236.7 17.2 %copy-start.8 = (f32[2048]{0:T(1024)S(1)}, f32[2048]{0:T(1024)}, u32[]{:S(2)}) copy-start(f32[2048]{0:T(1024)} %param.40) | copy-start | bytes 24580
  239.1 1.5 collective-permute-start
  241.2 9.6 %collective-permute-start.3 = (f32[16,2048]{1,0:T(8,128)S(1)}, f32[16,2048]{1,0:T(8,128)S(1)}, u32[]{:S(2)}, u32[]{:S(2)}) collective-permute-start(f32[16,2048]{1,0:T(8,128)S(1)} %fusion.116), channel_id=1, source_target_pairs={{0,6},{1,7},{2,4},{3,5},{4,2},{5,3},{6,0},{7,1},{8,14},{9,15},{10,... | collective-permute-start | bytes 393224 | tf_op jit(solution)/shard_map/ppermute | solution.py:106
  241.8 8.9 %collective-permute-start.2 = (f32[16,2048]{1,0:T(8,128)S(1)}, f32[16,2048]{1,0:T(8,128)S(1)}, u32[]{:S(2)}, u32[]{:S(2)}) collective-permute-start(f32[16,2048]{1,0:T(8,128)S(1)} %fusion.116), channel_id=1, source_target_pairs={{0,4},{1,5},{2,6},{3,7},{4,0},{5,1},{6,2},{7,3},{8,12},{9,13},{10,... | collective-permute-start | bytes 393224 | tf_op jit(solution)/shard_map/ppermute | solution.py:106
  243.2 8.9 %collective-permute-start.1 = (f32[16,2048]{1,0:T(8,128)S(1)}, f32[16,2048]{1,0:T(8,128)S(1)}, u32[]{:S(2)}, u32[]{:S(2)}) collective-permute-start(f32[16,2048]{1,0:T(8,128)S(1)} %fusion.116), channel_id=1, source_target_pairs={{0,2},{1,3},{2,0},{3,1},{4,6},{5,7},{6,4},{7,5},{8,10},{9,11},{10,... | collective-permute-start | bytes 393224 | tf_op jit(solution)/shard_map/ppermute | solution.py:106
  253.9 4.8 %collective-permute-start.6 = (bf16[9,2048]{1,0:T(8,128)(2,1)S(1)}, bf16[9,2048]{1,0:T(8,128)(2,1)S(1)}, u32[]{:S(2)}, u32[]{:S(2)}) collective-permute-start(bf16[9,2048]{1,0:T(8,128)(2,1)S(1)} %fusion.56), channel_id=1, source_target_pairs={{0,24},{8,16},{16,8},{24,0},{32,56},{40,48},{48,40},{56,32},{64,88... | collective-permute-start | bytes 110600 | tf_op jit(solution)/shard_map/ppermute | solution.py:106
  256.4 4.7 %collective-permute-start.5 = (bf16[9,2048]{1,0:T(8,128)(2,1)S(1)}, bf16[9,2048]{1,0:T(8,128)(2,1)S(1)}, u32[]{:S(2)}, u32[]{:S(2)}) collective-permute-start(bf16[9,2048]{1,0:T(8,128)(2,1)S(1)} %fusion.56), channel_id=1, source_target_pairs={{0,16},{8,24},{16,0},{24,8},{32,48},{40,56},{48,32},{56,40},{64,80... | collective-permute-start | bytes 110600 | tf_op jit(solution)/shard_map/ppermute | solution.py:106
  257.0 4.2 %collective-permute-start.4 = (bf16[9,2048]{1,0:T(8,128)(2,1)S(1)}, bf16[9,2048]{1,0:T(8,128)(2,1)S(1)}, u32[]{:S(2)}, u32[]{:S(2)}) collective-permute-start(bf16[9,2048]{1,0:T(8,128)(2,1)S(1)} %fusion.56), channel_id=1, source_target_pairs={{0,8},{8,0},{16,24},{24,16},{32,40},{40,32},{48,56},{56,48},{64,72... | collective-permute-start | bytes 110600 | tf_op jit(solution)/shard_map/ppermute | solution.py:106
  261.8 6.8 %collective-permute-start.9 = (bf16[36,2048]{1,0:T(8,128)(2,1)S(1)}, bf16[36,2048]{1,0:T(8,128)(2,1)S(1)}, u32[]{:S(2)}, u32[]{:S(2)}) collective-permute-start(bf16[36,2048]{1,0:T(8,128)(2,1)S(1)} %reshape.483), channel_id=1, source_target_pairs={{0,96},{8,104},{16,112},{24,120},{32,64},{40,72},{48,80},{56,88},{... | collective-permute-start | bytes 442376 | tf_op jit(solution)/shard_map/ppermute | solution.py:106
  264.6 5.7 %collective-permute-start.8 = (bf16[36,2048]{1,0:T(8,128)(2,1)S(1)}, bf16[36,2048]{1,0:T(8,128)(2,1)S(1)}, u32[]{:S(2)}, u32[]{:S(2)}) collective-permute-start(bf16[36,2048]{1,0:T(8,128)(2,1)S(1)} %reshape.483), channel_id=1, source_target_pairs={{0,64},{8,72},{16,80},{24,88},{32,96},{40,104},{48,112},{56,120},{... | collective-permute-start | bytes 442376 | tf_op jit(solution)/shard_map/ppermute | solution.py:106
  265.0 5.3 %collective-permute-start.7 = (bf16[36,2048]{1,0:T(8,128)(2,1)S(1)}, bf16[36,2048]{1,0:T(8,128)(2,1)S(1)}, u32[]{:S(2)}, u32[]{:S(2)}) collective-permute-start(bf16[36,2048]{1,0:T(8,128)(2,1)S(1)} %reshape.483), channel_id=1, source_target_pairs={{0,32},{8,40},{16,48},{24,56},{32,0},{40,8},{48,16},{56,24},{64,96... | collective-permute-start | bytes 442376 | tf_op jit(solution)/shard_map/ppermute | solution.py:106
  275.4 5.8 %collective-permute-start.10 = (f32[144]{0:T(256)S(1)}, f32[144]{0:T(256)S(1)}, u32[]{:S(2)}, u32[]{:S(2)}) collective-permute-start(f32[144]{0:T(256)S(1)} %convolution_reduce_fusion), channel_id=1, source_target_pairs={{0,1},{1,0},{2,3},{3,2},{4,5},{5,4},{6,7},{7,6},{8,9},{9,8},{10,11... | collective-permute-start | bytes 1736 | tf_op jit(solution)/shard_map/ppermute | solution.py:106
  281.8 4.2 %collective-permute-start.13 = (f32[144]{0:T(256)S(1)}, f32[144]{0:T(256)S(1)}, u32[]{:S(2)}, u32[]{:S(2)}) collective-permute-start(f32[144]{0:T(256)S(1)} %bitcast.167), channel_id=1, source_target_pairs={{0,6},{1,7},{2,4},{3,5},{4,2},{5,3},{6,0},{7,1},{8,14},{9,15},{10,... | collective-permute-start | bytes 1736 | tf_op jit(solution)/shard_map/ppermute | solution.py:106
  282.0 4.0 %collective-permute-start.12 = (f32[144]{0:T(256)S(1)}, f32[144]{0:T(256)S(1)}, u32[]{:S(2)}, u32[]{:S(2)}) collective-permute-start(f32[144]{0:T(256)S(1)} %bitcast.168), channel_id=1, source_target_pairs={{0,4},{1,5},{2,6},{3,7},{4,0},{5,1},{6,2},{7,3},{8,12},{9,13},{10,... | collective-permute-start | bytes 1736 | tf_op jit(solution)/shard_map/ppermute | solution.py:106
  284.0 2.9 collective-permute-start.11
  287.6 3.7 %collective-permute-start.16 = (f32[144]{0:T(256)S(1)}, f32[144]{0:T(256)S(1)}, u32[]{:S(2)}, u32[]{:S(2)}) collective-permute-start(f32[144]{0:T(256)S(1)} %bitcast.163), channel_id=1, source_target_pairs={{0,24},{8,16},{16,8},{24,0},{32,56},{40,48},{48,40},{56,32},{64,88... | collective-permute-start | bytes 1736 | tf_op jit(solution)/shard_map/ppermute | solution.py:106
  288.8 3.9 %collective-permute-start.15 = (f32[144]{0:T(256)S(1)}, f32[144]{0:T(256)S(1)}, u32[]{:S(2)}, u32[]{:S(2)}) collective-permute-start(f32[144]{0:T(256)S(1)} %bitcast.164), channel_id=1, source_target_pairs={{0,16},{8,24},{16,0},{24,8},{32,48},{40,56},{48,32},{56,40},{64,80... | collective-permute-start | bytes 1736 | tf_op jit(solution)/shard_map/ppermute | solution.py:106
  289.5 3.2 collective-permute-start.14
  292.7 3.7 %collective-permute-start.19 = (f32[144]{0:T(256)S(1)}, f32[144]{0:T(256)S(1)}, u32[]{:S(2)}, u32[]{:S(2)}) collective-permute-start(f32[144]{0:T(256)S(1)} %maximum_maximum_fusion.1), channel_id=1, source_target_pairs={{0,96},{8,104},{16,112},{24,120},{32,64},{40,72},{48,80},{56,88},{... | collective-permute-start | bytes 1736 | tf_op jit(solution)/shard_map/ppermute | solution.py:106
  294.9 3.9 %collective-permute-start.18 = (f32[144]{0:T(256)S(1)}, f32[144]{0:T(256)S(1)}, u32[]{:S(2)}, u32[]{:S(2)}) collective-permute-start(f32[144]{0:T(256)S(1)} %maximum_maximum_fusion.1), channel_id=1, source_target_pairs={{0,64},{8,72},{16,80},{24,88},{32,96},{40,104},{48,112},{56,120},{... | collective-permute-start | bytes 1736 | tf_op jit(solution)/shard_map/ppermute | solution.py:106
  295.2 3.5 %collective-permute-start.17 = (f32[144]{0:T(256)S(1)}, f32[144]{0:T(256)S(1)}, u32[]{:S(2)}, u32[]{:S(2)}) collective-permute-start(f32[144]{0:T(256)S(1)} %maximum_maximum_fusion.1), channel_id=1, source_target_pairs={{0,32},{8,40},{16,48},{24,56},{32,0},{40,8},{48,16},{56,24},{64,96... | collective-permute-start | bytes 1736 | tf_op jit(solution)/shard_map/ppermute | solution.py:106
  298.8 30.9 %copy-start.1 = (bf16[384,2048]{1,0:T(8,128)(2,1)S(1)}, bf16[384,2048]{1,0:T(8,128)(2,1)}, u32[]{:S(2)}) copy-start(bf16[384,2048]{1,0:T(8,128)(2,1)} %param.39) | copy-start | bytes 4718596
Sparse Core Ops, SparseCore 0:
  41.4 45.1 all-gather.8
  88.7 82.0 all-gather.4
  173.1 32.0 all-gather.6
  236.7 55.1 reduce-scatter.1
where the time goes:
time: 341 us; the launch traced here: 336 us
  waiting for transfers between devices  127 us (37%)
  matrix products  78.2 us (23%)
  starting transfers between devices  43.1 us (13%)
  local copies, waits for them, and re-layouts  26.2 us (8%)
  blocking collectives  23.8 us (7%)
  other arithmetic  22.4 us (7%)
  between operations  15.3 us (4%)
    all_gather x1, waiting for transfers between devices, shards(): lax.all_gather(pieces.reshape(tok_req, q_cols), 'kv', axis=1, tiled=True)  33.3 us
    ppermute x20, starting transfers between devices, radix_exchange(): got.append(lax.ppermute(value, axis, pairs))  25.5 us
    ppermute x20, waiting for transfers between devices, radix_exchange(): got.append(lax.ppermute(value, axis, pairs))  24.5 us
    all_to_all x1, blocking collectives, regroup(): lax.all_to_all(rows_in, ('req', 'kv'), split_axis=0, concat_axis=0, tiled...  23.8 us
    all_gather x1, waiting for transfers between devices, shards(): rows_all = lax.all_gather(owner_rows, 'kv', axis=0, tiled=True)  23.5 us
    all_to_all x1, waiting for transfers between devices, shards(): lax.all_to_all(jnp.broadcast_to(o_proj[None], (kv_count,) + o_proj.shape)...  20.7 us
    sub x1, matrix products, prefill_full(): expd = jnp.exp(scores - row_peak)  15.9 us
    dot_general x1, matrix products, shards(): jnp.dot(attended, o_full, preferred_element_type=jnp.float32)  14.6 us
  transfers between devices with their start and end apart: 26, of which 19 were waited for; matrix products, arithmetic and copies ran while one was open for 23% of the time, Pallas kernels for 0%

commit v1 on v0

--- a/solution.py
+++ b/solution.py
@@ -182,7 +182,12 @@
     slot_place = lax.dynamic_index_in_dim(slot_table, self_index, 0, keepdims=False) // rows_dev
     arrived = regroup(hidden_in[send_rows])
     owner_rows = arrived[slot_place]
-    rows_all = lax.all_gather(owner_rows, "kv", axis=0, tiled=True)
+    ring = [owner_rows]
+    for hop in range(7):
+        ring.append(lax.ppermute(ring[-1], "kv", [(dev, (dev + 1) % 8) for dev in range(8)]))
+    rows_all = jnp.roll(
+        jnp.concatenate(ring[::-1], axis=0), (lax.axis_index("kv") + 1) * ring[0].shape[0], axis=0
+    )
     normed = norm_rows(rows_all, attn_gain).astype(jnp.bfloat16)
     o_full = lax.all_to_all(
         jnp.broadcast_to(o_proj[None], (kv_count,) + o_proj.shape),

time: 341 us -> 425 us (1.25)
  waiting for transfers between devices: 127 us -> 185 us
  starting transfers between devices: 43.1 us -> 60.6 us
  local copies, waits for them, and re-layouts: 26.2 us -> 31.2 us
    ppermute x0 -> x7, waiting for transfers between devices: none -> 115 us  [shards(): lax.ppermute(ring[-1], 'kv', [(dev, (dev + 1) % 8) for dev in range(8)])]
    all_gather x1 -> x0, waiting for transfers between devices: 23.5 us -> none  [shards(): rows_all = lax.all_gather(owner_rows, 'kv', axis=0, tiled=True)]
    all_to_all x1, waiting for transfers between devices: 20.7 us -> 0.01 us  [shards(): lax.all_to_all(jnp.broadcast_to(o_proj[None], (kv_count,) + o_proj.shape)...]
    ppermute x0 -> x7, starting transfers between devices: none -> 15.1 us  [shards(): lax.ppermute(ring[-1], 'kv', [(dev, (dev + 1) % 8) for dev in range(8)])]
    all_gather x1, waiting for transfers between devices: 12.4 us -> 0.02 us  [shards(): weight_all = lax.all_gather(weight_piece, 'req', axis=1, tiled=True)]
    unnamed x49 -> x62, local copies, waits for them, and re-layouts: 4.74 us -> 11.6 us
  transfers between devices with their start and end apart: 26 -> 32, of which waited for: 19 -> 22; matrix products, arithmetic and copies ran while one was open for 23% -> 20% of each run, Pallas kernels for 0% -> 0%
where the time goes in v1:
time: 425 us; the launch traced here: 419 us
  waiting for transfers between devices  185 us (44%)
  matrix products  80.6 us (19%)
  starting transfers between devices  60.6 us (14%)
  local copies, waits for them, and re-layouts  31.2 us (7%)
  blocking collectives  23.8 us (6%)
  other arithmetic  22.1 us (5%)
  between operations  15.4 us (4%)
    ppermute x7, waiting for transfers between devices, shards(): lax.ppermute(ring[-1], 'kv', [(dev, (dev + 1) % 8) for dev in range(8)])  115 us
    all_gather x1, waiting for transfers between devices, shards(): lax.all_gather(pieces.reshape(tok_req, q_cols), 'kv', axis=1, tiled=True)  32.8 us
    ppermute x20, starting transfers between devices, radix_exchange(): got.append(lax.ppermute(value, axis, pairs))  25.5 us
    ppermute x20, waiting for transfers between devices, radix_exchange(): got.append(lax.ppermute(value, axis, pairs))  24.5 us
    all_to_all x1, blocking collectives, regroup(): lax.all_to_all(rows_in, ('req', 'kv'), split_axis=0, concat_axis=0, tiled...  23.8 us
    sub x1, matrix products, prefill_full(): expd = jnp.exp(scores - row_peak)  16 us
    ppermute x7, starting transfers between devices, shards(): lax.ppermute(ring[-1], 'kv', [(dev, (dev + 1) % 8) for dev in range(8)])  15.1 us
    dot_general x1, matrix products, shards(): jnp.dot(attended, o_full, preferred_element_type=jnp.float32)  14.5 us
  transfers between devices with their start and end apart: 32, of which 22 were waited for; matrix products, arithmetic and copies ran while one was open for 20% of the time, Pallas kernels for 0%

profile of v1, /device:TPU:1, one launch (start us, length us, event | category | flops | bytes accessed | tf_op | source)
XLA Modules:
  0.0 418.5 jit_solution(7780610250245038632)
XLA Ops:
  8.3 2.6 gather_fusion
  13.6 11.5 %all-to-all-start = ((bf16[128,2,1024]{2,1,0:T(2,128)(2,1)}), bf16[128,2,1024]{2,1,0:T(2,128)(2,1)S(1)}, u32[]{:S(2)}, u32[]{:S(2)}) async-start(bf16[128,2,1024]{2,1,0:T(2,128)(2,1)} %reshape.573), calls=%async_computation | async-start | bytes 1048576 | tf_op jit(solution)/shard_map/all_to_all | solution.py:147
  25.8 13.0 %all-to-all-done = bf16[128,2,1024]{2,1,0:T(2,128)(2,1)S(1)} async-done(((bf16[128,2,1024]{2,1,0:T(2,128)(2,1)}), bf16[128,2,1024]{2,1,0:T(2,128)(2,1)S(1)}, u32[]{:S(2)}, u32[]{:S(2)}) %all-to-all-start) | async-done | bytes 524320 | tf_op jit(solution)/shard_map/all_to_all | solution.py:147
  41.5 1.9 constant_dynamic-slice_fusion
  43.5 4.2 %collective-permute-done = bf16[128,2048]{1,0:T(8,128)(2,1)} collective-permute-done((bf16[128,2048]{1,0:T(8,128)(2,1)S(1)}, bf16[128,2048]{1,0:T(8,128)(2,1)}, u32[]{:S(2)}, u32[]{:S(2)}) %collective-permute-start) | collective-permute-done | bytes 524320 | tf_op jit(solution)/shard_map/ppermute | solution.py:187
  47.7 2.6 collective-permute-start.1
  51.6 5.1 %collective-permute-done.1 = bf16[128,2048]{1,0:T(8,128)(2,1)} collective-permute-done((bf16[128,2048]{1,0:T(8,128)(2,1)}, bf16[128,2048]{1,0:T(8,128)(2,1)}, u32[]{:S(2)}, u32[]{:S(2)}) %collective-permute-start.1) | collective-permute-done | bytes 524320 | tf_op jit(solution)/shard_map/ppermute | solution.py:187
  56.7 2.5 collective-permute-start.2
  59.2 6.4 %collective-permute-done.2 = bf16[128,2048]{1,0:T(8,128)(2,1)S(1)} collective-permute-done((bf16[128,2048]{1,0:T(8,128)(2,1)}, bf16[128,2048]{1,0:T(8,128)(2,1)S(1)}, u32[]{:S(2)}, u32[]{:S(2)}) %collective-permute-start.2) | collective-permute-done | bytes 524320 | tf_op jit(solution)/shard_map/ppermute | solution.py:187
  65.6 2.4 collective-permute-start.3
  68.0 5.6 %broadcast_in_dim.46 = bf16[8,256,2048]{2,1,0:T(8,128)(2,1)} broadcast(bf16[256,2048]{1,0:T(8,128)(2,1)} %param.35), dimensions={1,2} | broadcast | bytes 9437184 | tf_op jit(solution)/shard_map/broadcast_in_dim | solution.py:193
  73.6 8.4 %all-to-all-start.1 = ((bf16[8,256,2048]{2,1,0:T(8,128)(2,1)}), bf16[8,256,2048]{2,1,0:T(8,128)(2,1)}, u32[]{:S(2)}, u32[]{:S(2)}) async-start(bf16[8,256,2048]{2,1,0:T(8,128)(2,1)} %broadcast_in_dim.46), calls=%async_computation.1 | async-start | bytes 16777216 | tf_op jit(solution)/shard_map/all_to_all | solution.py:192
  82.7 1.6 collective-permute-start.4
  84.5 93.8 %collective-permute-done.4 = bf16[128,2048]{1,0:T(8,128)(2,1)S(1)} collective-permute-done((bf16[128,2048]{1,0:T(8,128)(2,1)S(1)}, bf16[128,2048]{1,0:T(8,128)(2,1)S(1)}, u32[]{:S(2)}, u32[]{:S(2)}) %collective-permute-start.4) | collective-permute-done | bytes 524320 | tf_op jit(solution)/shard_map/ppermute | solution.py:187
  178.3 2.5 collective-permute-start.5
  180.8 4.0 fusion.4
  184.8 2.1 collective-permute-done.5
  186.9 2.5 collective-permute-start.6
  189.4 3.2 multiply_cosine_fusion
  192.7 2.8 collective-permute-done.6
  202.5 2.5 copy-done.2
  206.7 3.7 multiply_reduce_fusion.1
  212.3 1.5 subtract_convert_fusion
  213.9 3.5 fusion.95
  218.1 3.6 convolution_convert_fusion
  221.7 2.9 fusion.61
  224.6 16.0 %fusion.96 = (f32[2,1016]{1,0:T(2,128)S(1)}, f32[2,1016,3064]{2,1,0:T(8,128)}) fusion(pred[1016,3064]{1,0:T(8,128)(4,1)} %fusion.4, bf16[1016,128]{1,0:T(8,128)(2,1)S(1)} %copy.49, bf16[2048,128]{1,0:T(8,128)(2,1)S(1)} %bitcast.175, bf16[1024,2,64]{2,0,1:T(8,128)(2,1)S(1)} %get-tuple-element.14, bf16[1024,2,64]{2,0,1:T(8,128)(2,1)S(1)} %get-tuple-element.15), kind=kOutput, calls=%fused_computation.204 | convolution fusion | flops 1621384704 | bytes 29334016 | tf_op jit(solution)/shard_map/sub | solution.py:48
  240.7 11.5 %fusion.32 = bf16[1016,2,128]{2,0,1:T(8,128)(2,1)S(1)} fusion(f32[2,1016,3064]{2,1,0:T(8,128)} %get-tuple-element.31, f32[2,1016]{1,0:T(2,128)S(1)} %get-tuple-element.30, bf16[1016,128]{1,0:T(8,128)(2,1)S(1)} %slice.142, bf16[2048,128]{1,0:T(8,128)(2,1)S(1)} %bitcast.176), kind=kOutput, calls=%fused_computation.50 | convolution fusion | flops 1608149248 | bytes 26216896 | tf_op jit(solution)/shard_map/gck,kd->cgd/dot_general | solution.py:50
  253.4 32.8 %all-gather.5.cloned.1.call-done = bf16[1024,2048]{0,1:T(8,128)(2,1)} async-done(((bf16[1024,256]{0,1:T(8,128)(2,1)}), bf16[1024,2048]{0,1:T(8,128)(2,1)}) %all-gather.5.cloned.1.call-update) | async-done | bytes 4194320 | tf_op jit(solution)/shard_map/all_gather | solution.py:257
  286.2 14.5 %fusion.7 = (f32[1024]{0:T(1024)S(1)}, bf16[1024,2048]{1,0:T(8,128)(2,1)S(1)}) fusion(bf16[1024,2048]{0,1:T(8,128)(2,1)} %all-gather.5.cloned.1.call-done, bf16[2048,2048]{1,0:T(8,128)(2,1)} %bitcast.25, bf16[2048,2048]{1,0:T(8,128)(2,1)} %copy-done.3, s32[]{:T(128)S(6)} %select_n.166), kind=kOutput, calls=%fused_computation.26 | convolution fusion | flops 8602516480 | bytes 20975620 | tf_op jit(solution)/shard_map/dot_general | solution.py:259
  300.8 7.0 %fusion.18 = f32[1024,768]{1,0:T(8,128)S(1)} fusion(bf16[3,768,2048]{2,1,0:T(8,128)(2,1)} %all-gather.3.cloned.1.call-done, bf16[1024,2048]{1,0:T(8,128)(2,1)S(1)} %get-tuple-element.33, f32[2048]{0:T(1024)S(1)} %copy-done.16, f32[1024]{0:T(1024)S(1)} %add_rsqrt_fusion.1), kind=kOutput, calls=%fused_computation.37 | convolution fusion | flops 3229614080 | bytes 10498048 | tf_op jit(solution)/shard_map/dot_general | solution.py:264
  307.9 3.9 multiply_convert_fusion
  312.9 5.7 %fusion.16 = f32[1024,2048]{1,0:T(8,128)} fusion(bf16[1024,768]{1,0:T(8,128)(2,1)S(1)} %multiply_convert_fusion, bf16[3,768,2048]{2,1,0:T(8,128)(2,1)S(1)} %bitcast.145), kind=kOutput, calls=%fused_computation.35 | convolution fusion | flops 3221225472 | bytes 13107200 | tf_op jit(solution)/shard_map/dot_general | solution.py:268
  318.8 2.4 fusion.14
  326.7 6.2 %collective-permute-done.10 = f32[16,2048]{1,0:T(8,128)S(1)} collective-permute-done((f32[16,2048]{1,0:T(8,128)S(1)}, f32[16,2048]{1,0:T(8,128)S(1)}, u32[]{:S(2)}, u32[]{:S(2)}) %collective-permute-start.10) | collective-permute-done | bytes 131104 | tf_op jit(solution)/shard_map/ppermute | solution.py:106
  336.0 2.5 collective-permute-start.13
  340.8 2.5 collective-permute-done.12
  344.0 2.8 collective-permute-start.16
  347.5 3.3 collective-permute-done.16
  350.8 1.7 collective-permute-done.15
  353.3 4.3 %convolution_reduce_fusion = f32[144]{0:T(256)S(1)} fusion(bf16[144,2048]{1,0:T(8,128)(2,1)S(1)} %reshape.484, bf16[2048,1187]{0,1:T(8,128)(2,1)} %param.41), kind=kOutput, calls=%fused_computation.52 | convolution fusion | flops 700291840 | bytes 5452352 | tf_op jit(solution)/shard_map/dot_general | solution.py:277
  357.6 5.0 %collective-permute-start.17 = (f32[144]{0:T(256)S(1)}, f32[144]{0:T(256)S(1)}, u32[]{:S(2)}, u32[]{:S(2)}) collective-permute-start(f32[144]{0:T(256)S(1)} %convolution_reduce_fusion), channel_id=1, source_target_pairs={{0,1},{1,0},{2,3},{3,2},{4,5},{5,4},{6,7},{7,6},{8,9},{9,8},{10,11... | collective-permute-start | bytes 1736 | tf_op jit(solution)/shard_map/ppermute | solution.py:106
  364.2 2.0 collective-permute-start.19
  374.9 2.1 collective-permute-start.26
  378.6 2.3 collective-permute-done.25
  381.5 2.3 scatter_custom_fusion
  385.2 23.8 %all_to_all.29 = bf16[128,2,1024]{2,1,0:T(2,128)(2,1)S(1)} all-to-all(bf16[128,2,1024]{2,1,0:T(2,128)(2,1)S(1)} %reshape.575), channel_id=1, replica_groups=mesh['req'=16,'kv'=8] {'req','kv'}, dimensions={0} | all-to-all | bytes 1048576 | tf_op jit(solution)/shard_map/all_to_all | solution.py:147
  409.4 2.4 scatter_custom_fusion.1
  (185 shorter events, 49.6 us)
Async XLA Ops:
  7.2 43.1 %copy-start = (bf16[384,2048]{1,0:T(8,128)(2,1)S(1)}, bf16[384,2048]{1,0:T(8,128)(2,1)}, u32[]{:S(2)}) copy-start(bf16[384,2048]{1,0:T(8,128)(2,1)} %param.39) | copy-start | bytes 4718596
  13.6 25.2 %all-to-all-start = ((bf16[128,2,1024]{2,1,0:T(2,128)(2,1)}), bf16[128,2,1024]{2,1,0:T(2,128)(2,1)S(1)}, u32[]{:S(2)}, u32[]{:S(2)}) async-start(bf16[128,2,1024]{2,1,0:T(2,128)(2,1)} %reshape.573), calls=%async_computation | async-start | bytes 1048576 | tf_op jit(solution)/shard_map/all_to_all | solution.py:147
  25.1 227.2 %all-gather.3.cloned.1.call-start = ((), (), s32[]{:S(2)}) async-start(), calls=%async_computation.4 | async-start | bytes 10027008 | tf_op jit(solution)/shard_map/all_gather | solution.py:208
  40.5 7.2 %collective-permute-start = (bf16[128,2048]{1,0:T(8,128)(2,1)S(1)}, bf16[128,2048]{1,0:T(8,128)(2,1)}, u32[]{:S(2)}, u32[]{:S(2)}) collective-permute-start(bf16[128,2048]{1,0:T(8,128)(2,1)S(1)} %gather_fusion.1), channel_id=1, source_target_pairs={{0,1},{1,2},{2,3},{3,4},{4,5},{5,6},{6,7},{7,0},{8,9},{9,10},{10,1... | collective-permute-start | bytes 1572872 | tf_op jit(solution)/shard_map/ppermute | solution.py:187
  47.7 9.0 %collective-permute-start.1 = (bf16[128,2048]{1,0:T(8,128)(2,1)}, bf16[128,2048]{1,0:T(8,128)(2,1)}, u32[]{:S(2)}, u32[]{:S(2)}) collective-permute-start(bf16[128,2048]{1,0:T(8,128)(2,1)} %collective-permute-done), channel_id=1, source_target_pairs={{0,1},{1,2},{2,3},{3,4},{4,5},{5,6},{6,7},{7,0},{8,9},{9,10},{10,1... | collective-permute-start | bytes 1572872 | tf_op jit(solution)/shard_map/ppermute | solution.py:187
  56.7 8.9 %collective-permute-start.2 = (bf16[128,2048]{1,0:T(8,128)(2,1)}, bf16[128,2048]{1,0:T(8,128)(2,1)S(1)}, u32[]{:S(2)}, u32[]{:S(2)}) collective-permute-start(bf16[128,2048]{1,0:T(8,128)(2,1)} %collective-permute-done.1), channel_id=1, source_target_pairs={{0,1},{1,2},{2,3},{3,4},{4,5},{5,6},{6,7},{7,0},{8,9},{9,10},{10,1... | collective-permute-start | bytes 1572872 | tf_op jit(solution)/shard_map/ppermute | solution.py:187
  65.6 17.1 %collective-permute-start.3 = (bf16[128,2048]{1,0:T(8,128)(2,1)S(1)}, bf16[128,2048]{1,0:T(8,128)(2,1)S(1)}, u32[]{:S(2)}, u32[]{:S(2)}) collective-permute-start(bf16[128,2048]{1,0:T(8,128)(2,1)S(1)} %collective-permute-done.2), channel_id=1, source_target_pairs={{0,1},{1,2},{2,3},{3,4},{4,5},{5,6},{6,7},{7,0},{8,9},{9,10},{10,1... | collective-permute-start | bytes 1572872 | tf_op jit(solution)/shard_map/ppermute | solution.py:187
  73.6 10.7 %copy-start.9 = (s32[8]{0:T(128)S(1)}, s32[8]{0:T(128)}, u32[]{:S(2)}) copy-start(s32[8]{0:T(128)} %param.23) | copy-start | bytes 100
  73.6 178.6 %all-to-all-start.1 = ((bf16[8,256,2048]{2,1,0:T(8,128)(2,1)}), bf16[8,256,2048]{2,1,0:T(8,128)(2,1)}, u32[]{:S(2)}, u32[]{:S(2)}) async-start(bf16[8,256,2048]{2,1,0:T(8,128)(2,1)} %broadcast_in_dim.46), calls=%async_computation.1 | async-start | bytes 16777216 | tf_op jit(solution)/shard_map/all_to_all | solution.py:192
  82.0 204.2 %all-gather.5.cloned.1.call-start = ((), (), s32[]{:S(2)}) async-start(), calls=%async_computation.5 | async-start | bytes 4718592 | tf_op jit(solution)/shard_map/all_gather | solution.py:257
  82.7 95.6 %collective-permute-start.4 = (bf16[128,2048]{1,0:T(8,128)(2,1)S(1)}, bf16[128,2048]{1,0:T(8,128)(2,1)S(1)}, u32[]{:S(2)}, u32[]{:S(2)}) collective-permute-start(bf16[128,2048]{1,0:T(8,128)(2,1)S(1)} %collective-permute-done.3), channel_id=1, source_target_pairs={{0,1},{1,2},{2,3},{3,4},{4,5},{5,6},{6,7},{7,0},{8,9},{9,10},{10,1... | collective-permute-start | bytes 1572872 | tf_op jit(solution)/shard_map/ppermute | solution.py:187
  178.3 8.6 %collective-permute-start.5 = (bf16[128,2048]{1,0:T(8,128)(2,1)S(1)}, bf16[128,2048]{1,0:T(8,128)(2,1)S(1)}, u32[]{:S(2)}, u32[]{:S(2)}) collective-permute-start(bf16[128,2048]{1,0:T(8,128)(2,1)S(1)} %collective-permute-done.4), channel_id=1, source_target_pairs={{0,1},{1,2},{2,3},{3,4},{4,5},{5,6},{6,7},{7,0},{8,9},{9,10},{10,1... | collective-permute-start | bytes 1572872 | tf_op jit(solution)/shard_map/ppermute | solution.py:187
  186.9 8.6 %collective-permute-start.6 = (bf16[128,2048]{1,0:T(8,128)(2,1)S(1)}, bf16[128,2048]{1,0:T(8,128)(2,1)S(1)}, u32[]{:S(2)}, u32[]{:S(2)}) collective-permute-start(bf16[128,2048]{1,0:T(8,128)(2,1)S(1)} %collective-permute-done.5), channel_id=1, source_target_pairs={{0,1},{1,2},{2,3},{3,4},{4,5},{5,6},{6,7},{7,0},{8,9},{9,10},{10,1... | collective-permute-start | bytes 1572872 | tf_op jit(solution)/shard_map/ppermute | solution.py:187
  195.7 5.7 %copy-start.8 = (f32[2048]{0:T(1024)S(1)}, f32[2048]{0:T(1024)}, u32[]{:S(2)}) copy-start(f32[2048]{0:T(1024)} %param.29) | copy-start | bytes 24580
  198.2 6.8 %copy-start.13 = (bf16[2048,256]{1,0:T(8,128)(2,1)S(1)}, bf16[2048,256]{1,0:T(8,128)(2,1)}, u32[]{:S(2)}) copy-start(bf16[2048,256]{1,0:T(8,128)(2,1)} %param.30) | copy-start | bytes 3145732
  200.5 5.8 %copy-start.3 = (bf16[2048,2048]{1,0:T(8,128)(2,1)}, bf16[2048,2048]{1,0:T(8,128)(2,1)S(1)}, u32[]{:S(2)}) copy-start(bf16[2048,2048]{1,0:T(8,128)(2,1)S(1)} %constant_dynamic-update-slice_fusion) | copy-start | bytes 25165828
  205.0 6.9 %copy-start.11 = (f32[128]{0:T(128)S(1)}, f32[128]{0:T(128)}, u32[]{:S(2)}) copy-start(f32[128]{0:T(128)} %param.33) | copy-start | bytes 1540
  206.3 5.9 %copy-start.4 = (f32[1024,64]{1,0:T(8,128)S(1)}, f32[1024,64]{1,0:T(8,128)}, u32[]{:S(2)}) copy-start(f32[1024,64]{1,0:T(8,128)} %get-tuple-element.22) | copy-start | bytes 786436
  213.9 10.7 %copy-start.14 = (bf16[1,2048,128]{2,1,0:T(8,128)(2,1)S(1)}, bf16[1,2048,128]{2,1,0:T(8,128)(2,1)}, u32[]{:S(2)}) copy-start(bf16[1,2048,128]{2,1,0:T(8,128)(2,1)} %param.27) | copy-start | bytes 1572868
  224.6 16.0 %copy-start.15 = (bf16[1,2048,128]{2,1,0:T(8,128)(2,1)S(1)}, bf16[1,2048,128]{2,1,0:T(8,128)(2,1)}, u32[]{:S(2)}) copy-start(bf16[1,2048,128]{2,1,0:T(8,128)(2,1)} %param.28) | copy-start | bytes 1572868
  253.3 47.5 %copy-start.16 = (f32[2048]{0:T(1024)S(1)}, f32[2048]{0:T(1024)}, u32[]{:S(2)}) copy-start(f32[2048]{0:T(1024)} %param.36) | copy-start | bytes 24580
  253.3 128.1 %reduce-scatter.2.cloned.1.call-start = ((), (), s32[]{:S(2)}) async-start(), calls=%async_computation.6 | async-start | bytes 9437184 | tf_op jit(solution)/shard_map/reduce_scatter | solution.py:269
  286.2 21.6 %slice-start = ((s8[9437184]{0:T(1024)(128)(4,1)}), s8[1048576]{0:T(1024)(128)(4,1)S(1)}, s32[]{:S(2)}) async-start(s8[9437184]{0:T(1024)(128)(4,1)} %bitcast.144), calls=%async_computation.7 | async-start | bytes 2097152
  286.2 21.6 %slice-start.1 = ((s8[9437184]{0:T(1024)(128)(4,1)}), s8[4194304]{0:T(1024)(128)(4,1)S(1)}, s32[]{:S(2)}) async-start(s8[9437184]{0:T(1024)(128)(4,1)} %bitcast.144), calls=%async_computation.8 | async-start | bytes 8388608
  300.8 7.1 %copy-start.6 = (bf16[1024,2048]{1,0:T(8,128)(2,1)}, bf16[1024,2048]{1,0:T(8,128)(2,1)S(1)}, u32[]{:S(2)}) copy-start(bf16[1024,2048]{1,0:T(8,128)(2,1)S(1)} %get-tuple-element.33) | copy-start | bytes 12582916
  300.8 7.1 %slice-start.2 = ((s8[9437184]{0:T(1024)(128)(4,1)}), s8[4194304]{0:T(1024)(128)(4,1)S(1)}, s32[]{:S(2)}) async-start(s8[9437184]{0:T(1024)(128)(4,1)} %bitcast.144), calls=%async_computation.9 | async-start | bytes 8388608
  318.6 17.3 %copy-start.7 = (f32[2048]{0:T(1024)S(1)}, f32[2048]{0:T(1024)}, u32[]{:S(2)}) copy-start(f32[2048]{0:T(1024)} %param.40) | copy-start | bytes 24580
  321.2 1.5 collective-permute-start.7
  323.3 9.6 %collective-permute-start.10 = (f32[16,2048]{1,0:T(8,128)S(1)}, f32[16,2048]{1,0:T(8,128)S(1)}, u32[]{:S(2)}, u32[]{:S(2)}) collective-permute-start(f32[16,2048]{1,0:T(8,128)S(1)} %fusion.116), channel_id=1, source_target_pairs={{0,6},{1,7},{2,4},{3,5},{4,2},{5,3},{6,0},{7,1},{8,14},{9,15},{10,... | collective-permute-start | bytes 393224 | tf_op jit(solution)/shard_map/ppermute | solution.py:106
  324.0 8.9 %collective-permute-start.9 = (f32[16,2048]{1,0:T(8,128)S(1)}, f32[16,2048]{1,0:T(8,128)S(1)}, u32[]{:S(2)}, u32[]{:S(2)}) collective-permute-start(f32[16,2048]{1,0:T(8,128)S(1)} %fusion.116), channel_id=1, source_target_pairs={{0,4},{1,5},{2,6},{3,7},{4,0},{5,1},{6,2},{7,3},{8,12},{9,13},{10,... | collective-permute-start | bytes 393224 | tf_op jit(solution)/shard_map/ppermute | solution.py:106
  325.4 8.9 %collective-permute-start.8 = (f32[16,2048]{1,0:T(8,128)S(1)}, f32[16,2048]{1,0:T(8,128)S(1)}, u32[]{:S(2)}, u32[]{:S(2)}) collective-permute-start(f32[16,2048]{1,0:T(8,128)S(1)} %fusion.116), channel_id=1, source_target_pairs={{0,2},{1,3},{2,0},{3,1},{4,6},{5,7},{6,4},{7,5},{8,10},{9,11},{10,... | collective-permute-start | bytes 393224 | tf_op jit(solution)/shard_map/ppermute | solution.py:106
  336.0 4.8 %collective-permute-start.13 = (bf16[9,2048]{1,0:T(8,128)(2,1)S(1)}, bf16[9,2048]{1,0:T(8,128)(2,1)S(1)}, u32[]{:S(2)}, u32[]{:S(2)}) collective-permute-start(bf16[9,2048]{1,0:T(8,128)(2,1)S(1)} %fusion.56), channel_id=1, source_target_pairs={{0,24},{8,16},{16,8},{24,0},{32,56},{40,48},{48,40},{56,32},{64,88... | collective-permute-start | bytes 110600 | tf_op jit(solution)/shard_map/ppermute | solution.py:106
  338.6 4.7 %collective-permute-start.12 = (bf16[9,2048]{1,0:T(8,128)(2,1)S(1)}, bf16[9,2048]{1,0:T(8,128)(2,1)S(1)}, u32[]{:S(2)}, u32[]{:S(2)}) collective-permute-start(bf16[9,2048]{1,0:T(8,128)(2,1)S(1)} %fusion.56), channel_id=1, source_target_pairs={{0,16},{8,24},{16,0},{24,8},{32,48},{40,56},{48,32},{56,40},{64,80... | collective-permute-start | bytes 110600 | tf_op jit(solution)/shard_map/ppermute | solution.py:106
  339.1 4.2 %collective-permute-start.11 = (bf16[9,2048]{1,0:T(8,128)(2,1)S(1)}, bf16[9,2048]{1,0:T(8,128)(2,1)S(1)}, u32[]{:S(2)}, u32[]{:S(2)}) collective-permute-start(bf16[9,2048]{1,0:T(8,128)(2,1)S(1)} %fusion.56), channel_id=1, source_target_pairs={{0,8},{8,0},{16,24},{24,16},{32,40},{40,32},{48,56},{56,48},{64,72... | collective-permute-start | bytes 110600 | tf_op jit(solution)/shard_map/ppermute | solution.py:106
  344.0 6.8 %collective-permute-start.16 = (bf16[36,2048]{1,0:T(8,128)(2,1)S(1)}, bf16[36,2048]{1,0:T(8,128)(2,1)S(1)}, u32[]{:S(2)}, u32[]{:S(2)}) collective-permute-start(bf16[36,2048]{1,0:T(8,128)(2,1)S(1)} %reshape.483), channel_id=1, source_target_pairs={{0,96},{8,104},{16,112},{24,120},{32,64},{40,72},{48,80},{56,88},{... | collective-permute-start | bytes 442376 | tf_op jit(solution)/shard_map/ppermute | solution.py:106
  346.7 5.8 %collective-permute-start.15 = (bf16[36,2048]{1,0:T(8,128)(2,1)S(1)}, bf16[36,2048]{1,0:T(8,128)(2,1)S(1)}, u32[]{:S(2)}, u32[]{:S(2)}) collective-permute-start(bf16[36,2048]{1,0:T(8,128)(2,1)S(1)} %reshape.483), channel_id=1, source_target_pairs={{0,64},{8,72},{16,80},{24,88},{32,96},{40,104},{48,112},{56,120},{... | collective-permute-start | bytes 442376 | tf_op jit(solution)/shard_map/ppermute | solution.py:106
  347.2 5.3 %collective-permute-start.14 = (bf16[36,2048]{1,0:T(8,128)(2,1)S(1)}, bf16[36,2048]{1,0:T(8,128)(2,1)S(1)}, u32[]{:S(2)}, u32[]{:S(2)}) collective-permute-start(bf16[36,2048]{1,0:T(8,128)(2,1)S(1)} %reshape.483), channel_id=1, source_target_pairs={{0,32},{8,40},{16,48},{24,56},{32,0},{40,8},{48,16},{56,24},{64,96... | collective-permute-start | bytes 442376 | tf_op jit(solution)/shard_map/ppermute | solution.py:106
  352.5 59.3 %copy-start.1 = (bf16[384,2048]{1,0:T(8,128)(2,1)S(1)}, bf16[384,2048]{1,0:T(8,128)(2,1)}, u32[]{:S(2)}) copy-start(bf16[384,2048]{1,0:T(8,128)(2,1)} %param.39) | copy-start | bytes 4718596
  357.6 5.8 %collective-permute-start.17 = (f32[144]{0:T(256)S(1)}, f32[144]{0:T(256)S(1)}, u32[]{:S(2)}, u32[]{:S(2)}) collective-permute-start(f32[144]{0:T(256)S(1)} %convolution_reduce_fusion), channel_id=1, source_target_pairs={{0,1},{1,0},{2,3},{3,2},{4,5},{5,4},{6,7},{7,6},{8,9},{9,8},{10,11... | collective-permute-start | bytes 1736 | tf_op jit(solution)/shard_map/ppermute | solution.py:106
  364.0 4.2 %collective-permute-start.20 = (f32[144]{0:T(256)S(1)}, f32[144]{0:T(256)S(1)}, u32[]{:S(2)}, u32[]{:S(2)}) collective-permute-start(f32[144]{0:T(256)S(1)} %bitcast.167), channel_id=1, source_target_pairs={{0,6},{1,7},{2,4},{3,5},{4,2},{5,3},{6,0},{7,1},{8,14},{9,15},{10,... | collective-permute-start | bytes 1736 | tf_op jit(solution)/shard_map/ppermute | solution.py:106
  364.2 4.0 collective-permute-start.19
  366.2 2.9 collective-permute-start.18
  369.7 3.7 collective-permute-start.23
  370.9 3.9 collective-permute-start.22
  371.7 3.2 collective-permute-start.21
  374.9 3.7 collective-permute-start.26
  377.0 3.9 collective-permute-start.25
  377.4 3.5 collective-permute-start.24
  (4 other events, 10.8 us)
Sparse Core Ops, SparseCore 0:
  51.7 73.2 all-gather.2
  253.4 32.7 all-gather.4
  318.8 55.1 reduce-scatter.1
